TPU v7x, 768 devices: a whole 4x8x12 slice. The times are simulated.
768 devices in a mesh: ctx: 192 (over z, y_hi, x, core), dp: 4 (over y_lo).
Axes of the slice: x: 4, y: 8 (y_hi: 2, y_lo: 4; y = y_hi * 4 + y_lo), z: 12, core: 2. Of those that a mesh axis runs over, the one named last changes fastest.
Arguments:
- queries: bfloat16 [98304, 4096], P(('dp', 'ctx')), parts along dimension 0, may hold values from -16 to 16
- key_rows: bfloat16 [98304, 4096], P(('dp', 'ctx')), parts along dimension 0, may hold values from -16 to 16
- value_rows: bfloat16 [98304, 4096], P(('dp', 'ctx')), parts along dimension 0, may hold values from -6 to 6
- lengths: int32 [512], P('dp'), parts along dimension 0, may hold values from 1 to 256, 24576 in all
- norm_gain: float32 [4096], replicated, may hold values from 0.1 to 1.9
- filters: bfloat16 [256, 128], replicated, may hold values from -0.5 to 0.5
- bypass: float32 [4096], replicated, may hold values from -4 to 4
Outputs:
- mixed: bfloat16 [98304, 4096], P(('dp', 'ctx')), parts along dimension 0
There are 4 independent parts, one for each index of `dp`. A program takes and returns all parts, laid end to end along the dimension named above; an argument that names none is the same for every part. Nothing has to cross between parts.
Inputs may be any that keep to these rules, and one draw needn't show every extreme that they name: The lengths sum to 24576; one of them is exactly 256.
All inputs are finite; a program needn't handle non-finite values.
Results may differ from a plain program's by a relative error of at most 0.012.
Values may be sent and summed in bfloat16 or wider, within the bound.
A program may use at most 32 MiB of HBM per device.

v0:
```python
import math

import jax
import jax.numpy as jnp
from jax import lax
from jax.sharding import PartitionSpec as P

HEAD_DIM = 128


def passed_along(x, axis, by):
    length = lax.axis_size(axis)
    pairs = [(i, i + by) for i in range(length) if 0 <= i + by < length]
    return lax.ppermute(x, axis, pairs)


def doc_starts(lengths, first_row, count):
    ends = jnp.cumsum(lengths)
    position = first_row + jnp.arange(count, dtype=jnp.int32)
    passed = ends[None, :] <= position[:, None]
    return jnp.sum(jnp.where(passed, lengths[None, :], 0), axis=1)


def attend(queries, key_block, value_block, key_first, starts, first_row):
    count = queries.shape[0]
    width = queries.shape[1]
    heads = width // HEAD_DIM
    span = key_block.shape[0]
    query_heads = queries.reshape(count, heads, HEAD_DIM)
    key_heads = key_block.reshape(span, heads, HEAD_DIM)
    value_heads = value_block.reshape(span, heads, HEAD_DIM)
    scores = jnp.einsum("thd,uhd->htu", query_heads, key_heads, preferred_element_type=jnp.float32)
    scores = scores * (1.0 / math.sqrt(HEAD_DIM))
    query_pos = first_row + jnp.arange(count, dtype=jnp.int32)
    key_pos = key_first + jnp.arange(span, dtype=jnp.int32)
    valid = (key_pos[None, :] >= starts[:, None]) & (key_pos[None, :] <= query_pos[:, None])
    scores = jnp.where(valid[None], scores, jnp.float32(-1e30))
    top = jnp.max(scores, axis=2, keepdims=True)
    raised = jnp.where(valid[None], jnp.exp(scores - top), jnp.float32(0.0))
    weights = (raised / jnp.sum(raised, axis=2, keepdims=True)).astype(jnp.bfloat16)
    result = jnp.einsum("htu,uhd->thd", weights, value_heads, preferred_element_type=jnp.float32)
    return result.astype(jnp.bfloat16).reshape(count, width)


def banded_conv(window, filters, out_first, out_starts):
    groups = filters.shape[0]
    taps = filters.shape[1]
    span = window.shape[0]
    count = span - taps + 1
    width = window.shape[1]
    group_size = width // groups
    in_position = out_first - (taps - 1) + jnp.arange(span, dtype=jnp.int32)
    keeper = (in_position[None, :] >= out_starts[:, None]).astype(jnp.bfloat16)
    block_size = math.gcd(groups, 32)
    grouped = jnp.transpose(window.reshape(span, groups, group_size), (1, 2, 0))

    def one_block(block_index):
        begin = block_index * block_size
        filter_block = lax.dynamic_slice_in_dim(filters, begin, block_size, 0)
        data_block = lax.dynamic_slice_in_dim(grouped, begin, block_size, 0)
        padded = jnp.concatenate(
            [filter_block[:, ::-1], jnp.zeros((block_size, count), filters.dtype)], axis=1
        )
        tiled = jnp.tile(padded, (1, count))[:, : count * span].reshape(block_size, count, span)
        matrix = tiled * keeper[None]
        return jnp.einsum("gts,gcs->gct", matrix, data_block, preferred_element_type=jnp.float32)

    pieces = lax.map(one_block, jnp.arange(groups // block_size, dtype=jnp.int32))
    joined = pieces.reshape(groups * group_size, count)
    return jnp.transpose(joined, (1, 0))


def shards(queries, key_rows, value_rows, lengths, norm_gain, filters, bypass):
    row_count = queries.shape[0]
    taps = filters.shape[1]
    first_row = lax.axis_index("ctx") * row_count
    starts = doc_starts(lengths, first_row, row_count)
    fetched = [passed_along((key_rows, value_rows), "ctx", offset) for offset in (2, 1)]
    far_keys, far_values = fetched[0]
    near_keys, near_values = fetched[1]
    all_keys = jnp.concatenate([far_keys, near_keys, key_rows], axis=0)
    all_values = jnp.concatenate([far_values, near_values, value_rows], axis=0)
    attended = attend(queries, all_keys, all_values, first_row - 2 * row_count, starts, first_row)
    attended32 = attended.astype(jnp.float32)
    squares = jnp.mean(attended32 * attended32, axis=1, keepdims=True)
    normed = (attended32 * lax.rsqrt(squares + 1e-06) * norm_gain[None, :]).astype(jnp.bfloat16)
    received = passed_along(normed[row_count - (taps - 1) :], "ctx", 1)
    window = jnp.concatenate([received, normed], axis=0)
    convolved = banded_conv(window, filters, first_row, starts)
    return (convolved + bypass[None, :] * normed.astype(jnp.float32)).astype(jnp.bfloat16)


def solution(mesh):
    in_specs = (
        P(("dp", "ctx"), None),
        P(("dp", "ctx"), None),
        P(("dp", "ctx"), None),
        P("dp"),
        P(),
        P(),
        P(),
    )
    out_specs = P(("dp", "ctx"), None)
    return jax.shard_map(shards, mesh=mesh, in_specs=in_specs, out_specs=out_specs, check_vma=False)
```

profile of v0, /device:TPU:552, one launch (start us, length us, event | category | flops | bytes accessed | tf_op | source)
XLA Modules:
  0.0 326.6 jit_solution(12468499553975879276)
XLA Ops:
  0.0 3.5 %collective-permute-start = (bf16[128,4096]{1,0:T(8,128)(2,1)}, bf16[128,4096]{1,0:T(8,128)(2,1)}, u32[]{:S(2)}, u32[]{:S(2)}) collective-permute-start(bf16[128,4096]{1,0:T(8,128)(2,1)} %param.11), channel_id=1, source_target_pairs={{0,8},{4,12},{8,16},{12,20},{16,24},{20,28},{24,32},{28,36},{32,40... | collective-permute-start | bytes 3145736 | tf_op jit(solution)/shard_map/ppermute | solution.py:14
  3.5 1.9 collective-permute-start.1
  5.5 1.6 copy.26
  7.1 3.4 %collective-permute-start.2 = (bf16[128,4096]{0,1:T(8,128)(2,1)S(1)}, bf16[128,4096]{0,1:T(8,128)(2,1)}, u32[]{:S(2)}, u32[]{:S(2)}) collective-permute-start(bf16[128,4096]{0,1:T(8,128)(2,1)S(1)} %copy.26), channel_id=1, source_target_pairs={{0,8},{4,12},{8,16},{12,20},{16,24},{20,28},{24,32},{28,36},{32,40... | collective-permute-start | bytes 3145736 | tf_op jit(solution)/shard_map/ppermute | solution.py:14
  10.5 2.9 collective-permute-start.3
  13.4 0.8 copy.25
  14.5 0.8 select_reduce_fusion
  15.5 50.0 %collective-permute-done = bf16[128,4096]{1,0:T(8,128)(2,1)} collective-permute-done((bf16[128,4096]{1,0:T(8,128)(2,1)}, bf16[128,4096]{1,0:T(8,128)(2,1)}, u32[]{:S(2)}, u32[]{:S(2)}) %collective-permute-start) | collective-permute-done | bytes 1048608 | tf_op jit(solution)/shard_map/ppermute | solution.py:14
  65.4 45.3 %collective-permute-done.1 = bf16[128,4096]{1,0:T(8,128)(2,1)} collective-permute-done((bf16[128,4096]{1,0:T(8,128)(2,1)}, bf16[128,4096]{1,0:T(8,128)(2,1)}, u32[]{:S(2)}, u32[]{:S(2)}) %collective-permute-start.1) | collective-permute-done | bytes 1048608 | tf_op jit(solution)/shard_map/ppermute | solution.py:14
  110.8 3.0 pad_maximum_fusion
  113.8 4.7 %copy.24 = bf16[384,4096]{0,1:T(8,128)(2,1)} copy(bf16[384,4096]{1,0:T(8,128)(2,1)} %pad_maximum_fusion) | data formatting | bytes 6291456 | tf_op jit(solution)/shard_map/concatenate | solution.py:82
  118.4 33.9 %collective-permute-done.3 = bf16[128,4096]{0,1:T(8,128)(2,1)} collective-permute-done((bf16[128,4096]{0,1:T(8,128)(2,1)S(1)}, bf16[128,4096]{0,1:T(8,128)(2,1)}, u32[]{:S(2)}, u32[]{:S(2)}) %collective-permute-start.3) | collective-permute-done | bytes 1048608 | tf_op jit(solution)/shard_map/ppermute | solution.py:14
  152.3 1.9 pad_maximum_fusion.1
  154.3 1.0 fusion.24
  155.3 2.4 fusion.29
  157.7 1.0 multiply_reduce_fusion
  158.8 1.3 copy-done.1
  160.1 0.8 fusion.21
  161.3 2.1 collective-permute-start.4
  163.4 33.4 %collective-permute-done.4 = bf16[127,4096]{0,1:T(8,128)(2,1)} collective-permute-done((bf16[127,4096]{0,1:T(8,128)(2,1)S(1)}, bf16[127,4096]{0,1:T(8,128)(2,1)}, u32[]{:S(2)}, u32[]{:S(2)}) %collective-permute-start.4) | collective-permute-done | bytes 1040416 | tf_op jit(solution)/shard_map/ppermute | solution.py:14
  196.8 3.4 %pad_maximum_fusion.2 = bf16[255,4096]{0,1:T(8,128)(2,1)} fusion(bf16[128,4096]{0,1:T(8,128)(2,1)S(1)} %fusion.21, bf16[127,4096]{0,1:T(8,128)(2,1)} %collective-permute-done.4), kind=kLoop, calls=%fused_computation.21 | loop fusion | flops 4177920 | bytes 4177920 | tf_op jit(solution)/shard_map/concatenate | solution.py:88
  200.2 122.2 %while.11 = (s32[]{:T(128)}, f32[8,32,16,128]{3,2,1,0:T(8,128)}, s32[8]{0:T(128)S(1)}, bf16[256,16,255]{2,1,0:T(8,128)(2,1)}, bf16[256,128]{1,0:T(8,128)(2,1)}, ...) while((s32[]{:T(128)}, f32[8,32,16,128]{3,2,1,0:T(8,128)}, ...), condition=%wide.region_6.7_spmd.clone, body=%wide.region_5.6_spmd.clone.sunk | while | flops 34533124 | bytes 17467060 | solution.py:68
  201.4 0.7 constant_dynamic-slice_fusion.2
  202.3 1.2 copy.42
  203.5 1.5 slice.11
  205.0 8.0 %reshape.142 = bf16[32,128,255]{2,1,0:T(8,128)(2,1)S(1)} reshape(bf16[32,32640]{1,0:T(8,128)(2,1)} %slice.11) | data formatting | bytes 4177920 | tf_op jit(solution)/shard_map/while/body/eval_jaxpr/reshape | solution.py:64
  213.1 2.3 fusion.38
  216.6 0.7 constant_dynamic-slice_fusion.2
  217.6 1.2 copy.42
  218.8 1.5 slice.11
  220.3 8.0 %reshape.142 = bf16[32,128,255]{2,1,0:T(8,128)(2,1)S(1)} reshape(bf16[32,32640]{1,0:T(8,128)(2,1)} %slice.11) | data formatting | bytes 4177920 | tf_op jit(solution)/shard_map/while/body/eval_jaxpr/reshape | solution.py:64
  228.4 2.3 fusion.38
  231.9 0.7 constant_dynamic-slice_fusion.2
  232.8 1.2 copy.42
  234.1 1.5 slice.11
  235.5 8.0 %reshape.142 = bf16[32,128,255]{2,1,0:T(8,128)(2,1)S(1)} reshape(bf16[32,32640]{1,0:T(8,128)(2,1)} %slice.11) | data formatting | bytes 4177920 | tf_op jit(solution)/shard_map/while/body/eval_jaxpr/reshape | solution.py:64
  243.7 2.3 fusion.38
  247.2 0.7 constant_dynamic-slice_fusion.2
  248.1 1.2 copy.42
  249.3 1.5 slice.11
  250.8 8.0 %reshape.142 = bf16[32,128,255]{2,1,0:T(8,128)(2,1)S(1)} reshape(bf16[32,32640]{1,0:T(8,128)(2,1)} %slice.11) | data formatting | bytes 4177920 | tf_op jit(solution)/shard_map/while/body/eval_jaxpr/reshape | solution.py:64
  258.9 2.3 fusion.38
  262.5 0.7 constant_dynamic-slice_fusion.2
  263.4 1.2 copy.42
  264.6 1.5 slice.11
  266.1 8.0 %reshape.142 = bf16[32,128,255]{2,1,0:T(8,128)(2,1)S(1)} reshape(bf16[32,32640]{1,0:T(8,128)(2,1)} %slice.11) | data formatting | bytes 4177920 | tf_op jit(solution)/shard_map/while/body/eval_jaxpr/reshape | solution.py:64
  274.2 2.3 fusion.38
  277.7 0.7 constant_dynamic-slice_fusion.2
  278.7 1.2 copy.42
  279.9 1.5 slice.11
  281.4 8.0 %reshape.142 = bf16[32,128,255]{2,1,0:T(8,128)(2,1)S(1)} reshape(bf16[32,32640]{1,0:T(8,128)(2,1)} %slice.11) | data formatting | bytes 4177920 | tf_op jit(solution)/shard_map/while/body/eval_jaxpr/reshape | solution.py:64
  289.5 2.3 fusion.38
  293.0 0.7 constant_dynamic-slice_fusion.2
  294.0 1.2 copy.42
  295.2 1.5 slice.11
  296.7 8.0 %reshape.142 = bf16[32,128,255]{2,1,0:T(8,128)(2,1)S(1)} reshape(bf16[32,32640]{1,0:T(8,128)(2,1)} %slice.11) | data formatting | bytes 4177920 | tf_op jit(solution)/shard_map/while/body/eval_jaxpr/reshape | solution.py:64
  304.8 2.3 fusion.38
  308.3 0.7 constant_dynamic-slice_fusion.2
  309.3 1.2 copy.42
  310.5 1.5 slice.11
  312.0 8.0 %reshape.142 = bf16[32,128,255]{2,1,0:T(8,128)(2,1)S(1)} reshape(bf16[32,32640]{1,0:T(8,128)(2,1)} %slice.11) | data formatting | bytes 4177920 | tf_op jit(solution)/shard_map/while/body/eval_jaxpr/reshape | solution.py:64
  320.1 2.3 fusion.38
  322.4 2.8 fusion.19
  325.2 1.3 copy.32
  (62 shorter events, 8.1 us)
Async XLA Ops:
  0.0 154.2 %copy-start = (bf16[128,4096]{1,0:T(8,128)(2,1)S(1)}, bf16[128,4096]{1,0:T(8,128)(2,1)}, u32[]{:S(2)}) copy-start(bf16[128,4096]{1,0:T(8,128)(2,1)} %param.9) | copy-start | bytes 3145732
  0.0 110.8 %copy-start.3 = (bf16[128,4096]{1,0:T(8,128)(2,1)S(1)}, bf16[128,4096]{1,0:T(8,128)(2,1)}, u32[]{:S(2)}) copy-start(bf16[128,4096]{1,0:T(8,128)(2,1)} %param.11) | copy-start | bytes 3145732
  0.0 65.4 %collective-permute-start = (bf16[128,4096]{1,0:T(8,128)(2,1)}, bf16[128,4096]{1,0:T(8,128)(2,1)}, u32[]{:S(2)}, u32[]{:S(2)}) collective-permute-start(bf16[128,4096]{1,0:T(8,128)(2,1)} %param.11), channel_id=1, source_target_pairs={{0,8},{4,12},{8,16},{12,20},{16,24},{20,28},{24,32},{28,36},{32,40... | collective-permute-start | bytes 3145736 | tf_op jit(solution)/shard_map/ppermute | solution.py:14
  3.5 107.2 %collective-permute-start.1 = (bf16[128,4096]{1,0:T(8,128)(2,1)}, bf16[128,4096]{1,0:T(8,128)(2,1)}, u32[]{:S(2)}, u32[]{:S(2)}) collective-permute-start(bf16[128,4096]{1,0:T(8,128)(2,1)} %param.11), channel_id=1, source_target_pairs={{0,4},{4,8},{8,12},{12,16},{16,20},{20,24},{24,28},{28,32},{32,36}... | collective-permute-start | bytes 3145736 | tf_op jit(solution)/shard_map/ppermute | solution.py:14
  7.1 111.4 %collective-permute-start.2 = (bf16[128,4096]{0,1:T(8,128)(2,1)S(1)}, bf16[128,4096]{0,1:T(8,128)(2,1)}, u32[]{:S(2)}, u32[]{:S(2)}) collective-permute-start(bf16[128,4096]{0,1:T(8,128)(2,1)S(1)} %copy.26), channel_id=1, source_target_pairs={{0,8},{4,12},{8,16},{12,20},{16,24},{20,28},{24,32},{28,36},{32,40... | collective-permute-start | bytes 3145736 | tf_op jit(solution)/shard_map/ppermute | solution.py:14
  10.5 141.8 %collective-permute-start.3 = (bf16[128,4096]{0,1:T(8,128)(2,1)S(1)}, bf16[128,4096]{0,1:T(8,128)(2,1)}, u32[]{:S(2)}, u32[]{:S(2)}) collective-permute-start(bf16[128,4096]{0,1:T(8,128)(2,1)S(1)} %copy.26), channel_id=1, source_target_pairs={{0,4},{4,8},{8,12},{12,16},{16,20},{20,24},{24,28},{28,32},{32,36}... | collective-permute-start | bytes 3145736 | tf_op jit(solution)/shard_map/ppermute | solution.py:14
  155.3 2.4 copy-start.2
  157.7 2.4 copy-start.4
  158.7 1.4 copy-start.1
  161.3 35.5 %collective-permute-start.4 = (bf16[127,4096]{0,1:T(8,128)(2,1)S(1)}, bf16[127,4096]{0,1:T(8,128)(2,1)}, u32[]{:S(2)}, u32[]{:S(2)}) collective-permute-start(bf16[127,4096]{0,1:T(8,128)(2,1)S(1)} %slice.9), channel_id=1, source_target_pairs={{0,4},{4,8},{8,12},{12,16},{16,20},{20,24},{24,28},{28,32},{32,36}... | collective-permute-start | bytes 3121160 | tf_op jit(solution)/shard_map/ppermute | solution.py:14
  200.2 122.2 %copy-start.5 = (f32[4096]{0:T(1024)S(1)}, f32[4096]{0:T(1024)}, u32[]{:S(2)}) copy-start(f32[4096]{0:T(1024)} %param.15) | copy-start | bytes 49156
where the time goes:
time: 328 us; the launch traced here: 327 us
  waiting for transfers between devices  162 us (49%)
  local copies, waits for them, and re-layouts  108 us (33%)
  matrix products  20.7 us (6%)
  other arithmetic  16.3 us (5%)
  starting transfers between devices  13.9 us (4%)
  loops' own time  4.88 us (1%)
    ppermute x5, waiting for transfers between devices, passed_along(): return lax.ppermute(x, axis, pairs)  162 us
    reshape x8, local copies, waits for them, and re-layouts, one_block(): jnp.tile(padded, (1, count))[:, :count * span]  64.3 us
    dot_general x8, matrix products, one_block(): jnp.einsum('gts,gcs->gct', matrix, data_block, preferred_element_type=jnp...  18.6 us
    ppermute x5, starting transfers between devices, passed_along(): return lax.ppermute(x, axis, pairs)  13.9 us
    slice x8, local copies, waits for them, and re-layouts, one_block(): jnp.tile(padded, (1, count))[:, :count * span]  11.8 us
    while x8, local copies, waits for them, and re-layouts  9.64 us
  transfers between devices with their start and end apart: 5, of which 4 were waited for; matrix products, arithmetic and copies ran while one was open for 3% of the time, Pallas kernels for 0%

commit v1 on v0

v1 whole, which is shorter than its diff:
```python
import functools
import math

import jax
import jax.numpy as jnp
from jax import lax
from jax.experimental import pallas as pl
from jax.experimental.pallas import tpu as pltpu
from jax.sharding import PartitionSpec as P

HEAD_DIM = 128
ROWS = 128
TAPS = 128
GROUP = 16
LANES = 128
F32 = jnp.float32
BF16 = jnp.bfloat16
EXPONENT = math.log2(math.e) / math.sqrt(HEAD_DIM)
MASKED = -1e30


def passed_along(x, axis, by):
    length = lax.axis_size(axis)
    pairs = [(i, i + by) for i in range(length) if 0 <= i + by < length]
    return lax.ppermute(x, axis, pairs)


def row_starts(lengths_row, first_row):
    docs = lengths_row.shape[1]
    upto = (
        lax.broadcasted_iota(jnp.int32, (docs, docs), 0) <= lax.broadcasted_iota(jnp.int32, (docs, docs), 1)
    ).astype(F32)
    sizes = jnp.broadcast_to(lengths_row.astype(F32), (8, docs))
    ends = jnp.dot(sizes.astype(BF16), upto.astype(BF16), preferred_element_type=F32)
    position = (first_row + lax.broadcasted_iota(jnp.int32, (ROWS, docs), 0)).astype(F32)
    passed = jnp.broadcast_to(ends[0:1], (ROWS, docs)) <= position
    return jnp.sum(jnp.where(passed, jnp.broadcast_to(sizes[0:1], (ROWS, docs)), 0.0), axis=1, keepdims=True)


def key_bias(starts, first_row, key_first, span):
    query_pos = (first_row + lax.broadcasted_iota(jnp.int32, (ROWS, span), 0)).astype(F32)
    key_pos = (key_first + lax.broadcasted_iota(jnp.int32, (ROWS, span), 1)).astype(F32)
    valid = (key_pos >= starts) & (key_pos <= query_pos)
    return jnp.where(valid, 0.0, MASKED)


def attend_head(query, keys, values, bias):
    scores = lax.dot_general(query, keys, (((1,), (1,)), ((), ())), preferred_element_type=F32) + bias
    top = jnp.max(scores, axis=1, keepdims=True)
    raised = jnp.exp2((scores - top) * EXPONENT)
    total = jnp.sum(raised, axis=1, keepdims=True)
    mixed = jnp.dot(raised.astype(BF16), values, preferred_element_type=F32)
    return mixed / total


def attention_kernel(lengths_ref, q_ref, k_ref, v_ref, kn_ref, vn_ref, kf_ref, vf_ref, o_ref, bias_ref):
    first_row = lax.axis_index("ctx") * ROWS
    starts = row_starts(lengths_ref[...], first_row)
    bias_ref[...] = key_bias(starts, first_row, first_row - 2 * ROWS, 3 * ROWS)

    def chunk(i, carry):
        for h in range(2):
            at = pl.ds(pl.multiple_of(i * 2 * HEAD_DIM + h * HEAD_DIM, HEAD_DIM), HEAD_DIM)
            keys = jnp.concatenate([kf_ref[:, at], kn_ref[:, at], k_ref[:, at]], axis=0)
            values = jnp.concatenate([vf_ref[:, at], vn_ref[:, at], v_ref[:, at]], axis=0)
            o_ref[:, at] = attend_head(q_ref[:, at], keys, values, bias_ref[...]).astype(BF16)
        return carry

    lax.fori_loop(0, q_ref.shape[1] // HEAD_DIM // 2, chunk, 0)


def filter_rows(filters):
    tap = lax.broadcasted_iota(jnp.int32, (TAPS, 2 * TAPS), 0)
    column = lax.broadcasted_iota(jnp.int32, (TAPS, 2 * TAPS), 1)
    place = (column == TAPS - tap).astype(F32).astype(BF16)
    return jnp.dot(filters, place, preferred_element_type=F32)


def build_block(base, keeper, index, matrix_ref):
    for g in range(LANES // GROUP):
        spread = jnp.broadcast_to(base[g : g + 1], (ROWS, 2 * TAPS))
        band = pltpu.roll(spread, 0, 1, stride=1, stride_axis=0)
        matrix_ref[index, :, g * 2 * TAPS : (g + 1) * 2 * TAPS] = (band * keeper).astype(BF16)


def window_keeper(starts, first_row):
    position = (first_row - TAPS + lax.broadcasted_iota(jnp.int32, (ROWS, 2 * TAPS), 1)).astype(F32)
    return (position >= starts).astype(F32)


def conv_block(matrix, window):
    group = lax.broadcasted_iota(jnp.int32, window.shape, 1) // GROUP
    parts = [jnp.where(group == g, window, jnp.zeros_like(window)) for g in range(LANES // GROUP)]
    return jnp.dot(matrix, jnp.concatenate(parts, axis=0), preferred_element_type=F32)


def row_scale(ref):
    blocks = ref.shape[1] // LANES
    total = jnp.zeros((ROWS, LANES), F32)
    for b in range(blocks):
        piece = ref[:, b * LANES : (b + 1) * LANES].astype(F32)
        total = total + piece * piece
    mean = jnp.sum(total, axis=1, keepdims=True) * (1.0 / ref.shape[1])
    return lax.rsqrt(mean + 1e-06)


def conv_kernel(lengths_ref, halo_ref, att_ref, gain_ref, filters_ref, bypass_ref, o_ref, base_ref, matrix_ref):
    first_row = lax.axis_index("ctx") * ROWS
    starts = row_starts(lengths_ref[...], first_row)
    keeper = window_keeper(starts, first_row)
    base_ref[...] = filter_rows(filters_ref[...])
    blocks = att_ref.shape[1] // LANES

    def build(i, carry):
        build_block(base_ref[pl.ds(pl.multiple_of(i * 8, 8), 8), :], keeper, i, matrix_ref)
        return carry

    lax.fori_loop(0, blocks, build, 0)
    near_scale = row_scale(att_ref)
    far_scale = row_scale(halo_ref)

    def mix(i, carry):
        at = pl.ds(pl.multiple_of(i * LANES, LANES), LANES)
        gain = gain_ref[:, at]
        near = (att_ref[:, at].astype(F32) * near_scale * gain).astype(BF16)
        far = (halo_ref[:, at].astype(F32) * far_scale * gain).astype(BF16)
        summed = conv_block(matrix_ref[i], jnp.concatenate([far, near], axis=0))
        o_ref[:, at] = (summed + bypass_ref[:, at] * near.astype(F32)).astype(BF16)
        return carry

    lax.fori_loop(0, blocks, mix, 0)


def shards(queries, key_rows, value_rows, lengths, norm_gain, filters, bypass):
    width = queries.shape[1]
    vmem = pl.BlockSpec(memory_space=pltpu.VMEM)
    lengths = lengths.reshape(1, -1)
    near_keys, near_values = passed_along((key_rows, value_rows), "ctx", 1)
    far_keys, far_values = passed_along((key_rows, value_rows), "ctx", 2)
    attended = pl.pallas_call(
        attention_kernel,
        out_shape=jax.ShapeDtypeStruct((ROWS, width), BF16),
        in_specs=[vmem] * 8,
        out_specs=vmem,
        scratch_shapes=[pltpu.VMEM((ROWS, 3 * ROWS), F32)],
        name="attention",
    )(lengths, queries, key_rows, value_rows, near_keys, near_values, far_keys, far_values)
    halo = passed_along(attended, "ctx", 1)
    return pl.pallas_call(
        conv_kernel,
        out_shape=jax.ShapeDtypeStruct((ROWS, width), BF16),
        in_specs=[vmem] * 6,
        out_specs=vmem,
        scratch_shapes=[
            pltpu.VMEM((filters.shape[0], 2 * TAPS), F32),
            pltpu.VMEM((width // LANES, ROWS, LANES // GROUP * 2 * TAPS), BF16),
        ],
        compiler_params=pltpu.CompilerParams(vmem_limit_bytes=48 * 2**20),
        name="conv",
    )(lengths, halo, attended, norm_gain.reshape(1, -1), filters, bypass.reshape(1, -1))


def solution(mesh):
    rows = P(("dp", "ctx"), None)
    return jax.shard_map(
        shards, mesh=mesh, in_specs=(rows, rows, rows, P("dp"), P(), P(), P()), out_specs=rows, check_vma=False
    )
```

time: 328 us -> 217 us (0.66)
  local copies, waits for them, and re-layouts: 108 us -> 3.19 us
  Pallas kernels: 0 us -> 37.2 us
  matrix products: 20.7 us -> 0 us
  waiting for transfers between devices: 162 us -> 145 us
  starting transfers between devices: 13.9 us -> 30.7 us
  other arithmetic: 16.3 us -> 0 us
  loops' own time: 4.88 us -> 0 us
    reshape x8 -> x0, local copies, waits for them, and re-layouts: 64.3 us -> none  [one_block(): jnp.tile(padded, (1, count))[:, :count * span]]
    pallas_call x0 -> x2, Pallas kernels: none -> 37.2 us  [the longest x1 22.1 us: shards(): pl.pallas_call(conv_kernel, out_shape=jax.ShapeDtypeStruct((ROWS, width),...]
    dot_general x10 -> x0, matrix products: 20.7 us -> none  [the longest x8 18.6 us: one_block(): jnp.einsum('gts,gcs->gct', matrix, data_block, preferred_element_type=jnp...]
    ppermute x5, waiting for transfers between devices: 162 us -> 145 us  [passed_along(): return lax.ppermute(x, axis, pairs)]
    ppermute x5, starting transfers between devices: 13.9 us -> 30.7 us  [passed_along(): return lax.ppermute(x, axis, pairs)]
    slice x9 -> x0, local copies, waits for them, and re-layouts: 12.2 us -> none  [the longest x8 11.8 us: one_block(): jnp.tile(padded, (1, count))[:, :count * span]]
    dynamic_slice x16 -> x0, local copies, waits for them, and re-layouts: 10.3 us -> none  [the longest x8 5.64 us: one_block(): filter_block = lax.dynamic_slice_in_dim(filters, begin, block_size, 0)]
    while x8 -> x0, local copies, waits for them, and re-layouts: 9.64 us -> none
  transfers between devices with their start and end apart: 5 -> 5, of which waited for: 4 -> 4; matrix products, arithmetic and copies ran while one was open for 3% -> 0% of each run, Pallas kernels for 0% -> 0%
where the time goes in v1:
time: 217 us
  waiting for transfers between devices  145 us (67%)
  Pallas kernels  37.2 us (17%)
  starting transfers between devices  30.7 us (14%)
  local copies, waits for them, and re-layouts  3.19 us (1%)
    ppermute x5, waiting for transfers between devices, passed_along(): return lax.ppermute(x, axis, pairs)  145 us
    ppermute x5, starting transfers between devices, passed_along(): return lax.ppermute(x, axis, pairs)  30.7 us
    pallas_call x1, Pallas kernels, shards(): pl.pallas_call(conv_kernel, out_shape=jax.ShapeDtypeStruct((ROWS, width),...  22.1 us
    pallas_call x1, Pallas kernels, shards(): pl.pallas_call(attention_kernel, out_shape=jax.ShapeDtypeStruct((ROWS, wi...  15.1 us
  transfers between devices with their start and end apart: 5, of which 4 were waited for; matrix products, arithmetic and copies ran while one was open for 0% of the time, Pallas kernels for 0%

profile of v1, /device:TPU:552, one launch (start us, length us, event | category | flops | bytes accessed | tf_op | source)
XLA Modules:
  0.0 216.6 jit_solution(12311082176648227791)
XLA Ops:
  0.0 1.9 collective-permute-start
  1.9 3.4 %collective-permute-start.2 = (bf16[128,4096]{1,0:T(8,128)(2,1)}, bf16[128,4096]{1,0:T(8,128)(2,1)S(1)}, u32[]{:S(2)}, u32[]{:S(2)}) collective-permute-start(bf16[128,4096]{1,0:T(8,128)(2,1)} %k_ref.1), channel_id=1, source_target_pairs={{0,8},{4,12},{8,16},{12,20},{16,24},{20,28},{24,32},{28,36},{32,40... | collective-permute-start | bytes 3145736 | tf_op jit(solution)/shard_map/ppermute | solution.py:25
  5.3 3.2 %collective-permute-start.1 = (bf16[128,4096]{1,0:T(8,128)(2,1)}, bf16[128,4096]{1,0:T(8,128)(2,1)S(1)}, u32[]{:S(2)}, u32[]{:S(2)}) collective-permute-start(bf16[128,4096]{1,0:T(8,128)(2,1)} %v_ref.1), channel_id=1, source_target_pairs={{0,4},{4,8},{8,12},{12,16},{16,20},{20,24},{24,28},{28,32},{32,36}... | collective-permute-start | bytes 3145736 | tf_op jit(solution)/shard_map/ppermute | solution.py:25
  8.6 3.1 %collective-permute-start.3 = (bf16[128,4096]{1,0:T(8,128)(2,1)}, bf16[128,4096]{1,0:T(8,128)(2,1)S(1)}, u32[]{:S(2)}, u32[]{:S(2)}) collective-permute-start(bf16[128,4096]{1,0:T(8,128)(2,1)} %v_ref.1), channel_id=1, source_target_pairs={{0,8},{4,12},{8,16},{12,20},{16,24},{20,28},{24,32},{28,36},{32,40... | collective-permute-start | bytes 3145736 | tf_op jit(solution)/shard_map/ppermute | solution.py:25
  11.7 52.9 %collective-permute-done.kn_ref = bf16[128,4096]{1,0:T(8,128)(2,1)S(1)} collective-permute-done((bf16[128,4096]{1,0:T(8,128)(2,1)}, bf16[128,4096]{1,0:T(8,128)(2,1)S(1)}, u32[]{:S(2)}, u32[]{:S(2)}) %collective-permute-start) | collective-permute-done | bytes 1048608 | tf_op jit(solution)/shard_map/ppermute | solution.py:25
  64.6 0.0 copy-start.5
  64.6 1.2 collective-permute-done.2.kf_ref
  65.8 0.0 copy-start.6
  65.8 69.2 %collective-permute-done.1.vn_ref = bf16[128,4096]{1,0:T(8,128)(2,1)S(1)} collective-permute-done((bf16[128,4096]{1,0:T(8,128)(2,1)}, bf16[128,4096]{1,0:T(8,128)(2,1)S(1)}, u32[]{:S(2)}, u32[]{:S(2)}) %collective-permute-start.1) | collective-permute-done | bytes 1048608 | tf_op jit(solution)/shard_map/ppermute | solution.py:25
  135.0 0.0 copy-start.7
  135.0 0.0 collective-permute-done.3.vf_ref
  135.0 0.0 copy-start.8
  135.0 1.0 copy-done.8
  136.0 0.0 copy-done.5
  136.0 0.0 copy-done.6
  136.0 0.3 copy-done.7
  136.3 0.0 copy-start.1
  136.3 0.0 copy-start.2
  136.3 0.0 copy-start.3
  136.3 15.1 %attention.1.att_ref = bf16[128,4096]{1,0:T(8,128)(2,1)} custom-call(s32[1,128]{1,0:T(1,128)} %bitcast.5, bf16[128,4096]{1,0:T(8,128)(2,1)} %q_ref.1, bf16[128,4096]{1,0:T(8,128)(2,1)} %k_ref.1, bf16[128,4096]{1,0:T(8,128)(2,1)} %v_ref.1, bf16[128,4096]{1,0:T(8,128)(2,1)} %copy-done.5, bf16[128,4096]{1,0:T(8,128)(2,1)} %copy-done.7, ...), custom_call_target="tpu_custom_call" | custom-call | tf_op jit(solution)/shard_map/attention/pallas_call | solution.py:140
  151.4 19.1 %collective-permute-start.4 = (bf16[128,4096]{1,0:T(8,128)(2,1)}, bf16[128,4096]{1,0:T(8,128)(2,1)S(1)}, u32[]{:S(2)}, u32[]{:S(2)}) collective-permute-start(bf16[128,4096]{1,0:T(8,128)(2,1)} %attention.1.att_ref), channel_id=1, source_target_pairs={{0,4},{4,8},{8,12},{12,16},{16,20},{20,24},{24,28},{28,32},{32,36}... | collective-permute-start | bytes 3145736 | tf_op jit(solution)/shard_map/ppermute | solution.py:25
  170.4 22.2 %collective-permute-done.4.halo_ref = bf16[128,4096]{1,0:T(8,128)(2,1)S(1)} collective-permute-done((bf16[128,4096]{1,0:T(8,128)(2,1)}, bf16[128,4096]{1,0:T(8,128)(2,1)S(1)}, u32[]{:S(2)}, u32[]{:S(2)}) %collective-permute-start.4) | collective-permute-done | bytes 1048608 | tf_op jit(solution)/shard_map/ppermute | solution.py:25
  192.6 0.0 copy-start.4
  192.6 0.0 copy-done.1
  192.6 0.0 copy-done.2
  192.6 0.0 copy-done.3
  192.6 0.6 copy-done.4
  193.3 0.0 copy-start
  193.3 1.2 copy-done
  194.5 22.1 %conv.1 = bf16[128,4096]{1,0:T(8,128)(2,1)} custom-call(s32[1,128]{1,0:T(1,128)S(1)} %bitcast.6, bf16[128,4096]{1,0:T(8,128)(2,1)S(1)} %collective-permute-done.4.halo_ref, bf16[128,4096]{1,0:T(8,128)(2,1)S(1)} %copy-done, f32[1,4096]{1,0:T(1,128)S(1)} %bitcast.3, bf16[256,128]{1,0:T(8,128)(2,1)S(1)} %copy-done.1, f32[1,4096]{1,0:T(1,128)S(1)} %bitcast.4), custom_call_target="tpu_custom_call" | custom-call | tf_op jit(solution)/shard_map/conv/pallas_call | solution.py:149
Async XLA Ops:
  0.0 64.6 %collective-permute-start = (bf16[128,4096]{1,0:T(8,128)(2,1)}, bf16[128,4096]{1,0:T(8,128)(2,1)S(1)}, u32[]{:S(2)}, u32[]{:S(2)}) collective-permute-start(bf16[128,4096]{1,0:T(8,128)(2,1)} %k_ref.1), channel_id=1, source_target_pairs={{0,4},{4,8},{8,12},{12,16},{16,20},{20,24},{24,28},{28,32},{32,36}... | collective-permute-start | bytes 3145736 | tf_op jit(solution)/shard_map/ppermute | solution.py:25
  1.9 63.8 %collective-permute-start.2 = (bf16[128,4096]{1,0:T(8,128)(2,1)}, bf16[128,4096]{1,0:T(8,128)(2,1)S(1)}, u32[]{:S(2)}, u32[]{:S(2)}) collective-permute-start(bf16[128,4096]{1,0:T(8,128)(2,1)} %k_ref.1), channel_id=1, source_target_pairs={{0,8},{4,12},{8,16},{12,20},{16,24},{20,28},{24,32},{28,36},{32,40... | collective-permute-start | bytes 3145736 | tf_op jit(solution)/shard_map/ppermute | solution.py:25
  5.3 129.6 %collective-permute-start.1 = (bf16[128,4096]{1,0:T(8,128)(2,1)}, bf16[128,4096]{1,0:T(8,128)(2,1)S(1)}, u32[]{:S(2)}, u32[]{:S(2)}) collective-permute-start(bf16[128,4096]{1,0:T(8,128)(2,1)} %v_ref.1), channel_id=1, source_target_pairs={{0,4},{4,8},{8,12},{12,16},{16,20},{20,24},{24,28},{28,32},{32,36}... | collective-permute-start | bytes 3145736 | tf_op jit(solution)/shard_map/ppermute | solution.py:25
  8.6 126.4 %collective-permute-start.3 = (bf16[128,4096]{1,0:T(8,128)(2,1)}, bf16[128,4096]{1,0:T(8,128)(2,1)S(1)}, u32[]{:S(2)}, u32[]{:S(2)}) collective-permute-start(bf16[128,4096]{1,0:T(8,128)(2,1)} %v_ref.1), channel_id=1, source_target_pairs={{0,8},{4,12},{8,16},{12,20},{16,24},{20,28},{24,32},{28,36},{32,40... | collective-permute-start | bytes 3145736 | tf_op jit(solution)/shard_map/ppermute | solution.py:25
  64.6 71.4 %copy-start.5 = (bf16[128,4096]{1,0:T(8,128)(2,1)}, bf16[128,4096]{1,0:T(8,128)(2,1)S(1)}, u32[]{:S(2)}) copy-start(bf16[128,4096]{1,0:T(8,128)(2,1)S(1)} %collective-permute-done.kn_ref) | copy-start | bytes 3145732
  65.8 70.2 %copy-start.6 = (bf16[128,4096]{1,0:T(8,128)(2,1)}, bf16[128,4096]{1,0:T(8,128)(2,1)S(1)}, u32[]{:S(2)}) copy-start(bf16[128,4096]{1,0:T(8,128)(2,1)S(1)} %collective-permute-done.2.kf_ref) | copy-start | bytes 3145732
  135.0 1.3 copy-start.7
  135.0 1.0 copy-start.8
  136.3 56.4 %copy-start.1 = (bf16[256,128]{1,0:T(8,128)(2,1)S(1)}, bf16[256,128]{1,0:T(8,128)(2,1)}, u32[]{:S(2)}) copy-start(bf16[256,128]{1,0:T(8,128)(2,1)} %filters_ref.1) | copy-start | bytes 196612
  136.3 56.4 %copy-start.2 = (f32[4096]{0:T(1024)S(1)}, f32[4096]{0:T(1024)}, u32[]{:S(2)}) copy-start(f32[4096]{0:T(1024)} %param.11) | copy-start | bytes 49156
  136.3 56.4 %copy-start.3 = (f32[4096]{0:T(1024)S(1)}, f32[4096]{0:T(1024)}, u32[]{:S(2)}) copy-start(f32[4096]{0:T(1024)} %param.13) | copy-start | bytes 49156
  151.4 41.3 %collective-permute-start.4 = (bf16[128,4096]{1,0:T(8,128)(2,1)}, bf16[128,4096]{1,0:T(8,128)(2,1)S(1)}, u32[]{:S(2)}, u32[]{:S(2)}) collective-permute-start(bf16[128,4096]{1,0:T(8,128)(2,1)} %attention.1.att_ref), channel_id=1, source_target_pairs={{0,4},{4,8},{8,12},{12,16},{16,20},{20,24},{24,28},{28,32},{32,36}... | collective-permute-start | bytes 3145736 | tf_op jit(solution)/shard_map/ppermute | solution.py:25
  192.6 0.7 copy-start.4
  193.3 1.2 copy-start

commit v2 on v1

v2 whole, which is shorter than its diff:
```python
import functools
import math

import jax
import jax.numpy as jnp
from jax import lax
from jax.experimental import pallas as pl
from jax.experimental.pallas import tpu as pltpu
from jax.sharding import PartitionSpec as P

HEAD_DIM = 128
ROWS = 128
TAPS = 128
GROUP = 16
LANES = 128
STATS = 16
CHUNK_HEADS = 2
WIDTH = CHUNK_HEADS * HEAD_DIM
AHEAD = 4
F32 = jnp.float32
BF16 = jnp.bfloat16
EXPONENT = math.log2(math.e) / math.sqrt(HEAD_DIM)
MASKED = -1e30
MESH = pl.DeviceIdType.MESH


def row_starts(lengths_row, first_row):
    docs = lengths_row.shape[1]
    upto = (
        lax.broadcasted_iota(jnp.int32, (docs, docs), 0) <= lax.broadcasted_iota(jnp.int32, (docs, docs), 1)
    ).astype(F32)
    sizes = jnp.broadcast_to(lengths_row.astype(F32), (8, docs))
    ends = jnp.dot(sizes.astype(BF16), upto.astype(BF16), preferred_element_type=F32)
    position = (first_row + lax.broadcasted_iota(jnp.int32, (ROWS, docs), 0)).astype(F32)
    passed = jnp.broadcast_to(ends[0:1], (ROWS, docs)) <= position
    return jnp.sum(jnp.where(passed, jnp.broadcast_to(sizes[0:1], (ROWS, docs)), 0.0), axis=1, keepdims=True)


def key_bias(starts, first_row, key_first, span):
    query_pos = (first_row + lax.broadcasted_iota(jnp.int32, (ROWS, span), 0)).astype(F32)
    key_pos = (key_first + lax.broadcasted_iota(jnp.int32, (ROWS, span), 1)).astype(F32)
    valid = (key_pos >= starts) & (key_pos <= query_pos)
    return jnp.where(valid, 0.0, MASKED)


def attend(query, keys, values, bias):
    scores = lax.dot_general(query, keys, (((1,), (1,)), ((), ())), preferred_element_type=F32) + bias
    top = jnp.max(scores, axis=1, keepdims=True)
    raised = jnp.exp2((scores - top) * EXPONENT)
    total = jnp.sum(raised, axis=1, keepdims=True)
    return jnp.dot(raised.astype(BF16), values, preferred_element_type=F32), total, top


def diagonal():
    return lax.broadcasted_iota(jnp.int32, (ROWS, ROWS), 0) == lax.broadcasted_iota(jnp.int32, (ROWS, ROWS), 1)


def pieces_of(column):
    row = jnp.sum(jnp.where(diagonal(), jnp.broadcast_to(column, (ROWS, ROWS)), 0.0), axis=0, keepdims=True)
    high = row.astype(BF16).astype(F32)
    middle = (row - high).astype(BF16).astype(F32)
    low = row - high - middle
    index = lax.broadcasted_iota(jnp.int32, (STATS, ROWS), 0)
    shape = (STATS, ROWS)
    rest = jnp.where(index == 2, jnp.broadcast_to(low, shape), 0.0)
    rest = jnp.where(index == 1, jnp.broadcast_to(middle, shape), rest)
    return jnp.where(index == 0, jnp.broadcast_to(high, shape), rest).astype(BF16)


def column_of(pieces):
    row = jnp.sum(pieces.astype(F32), axis=0, keepdims=True)
    return jnp.sum(jnp.where(diagonal(), jnp.broadcast_to(row, (ROWS, ROWS)), 0.0), axis=1, keepdims=True)


def filter_rows(filters):
    tap = lax.broadcasted_iota(jnp.int32, (TAPS, 2 * TAPS), 0)
    column = lax.broadcasted_iota(jnp.int32, (TAPS, 2 * TAPS), 1)
    place = (column == TAPS - tap).astype(F32).astype(BF16)
    return jnp.dot(filters, place, preferred_element_type=F32)


def build_block(base, keeper, index, matrix_ref):
    for g in range(LANES // GROUP):
        spread = jnp.broadcast_to(base[g : g + 1], (ROWS, 2 * TAPS))
        band = pltpu.roll(spread, 0, 1, stride=1, stride_axis=0)
        matrix_ref[index, :, g * 2 * TAPS : (g + 1) * 2 * TAPS] = (band * keeper).astype(BF16)


def window_keeper(starts, first_row):
    position = (first_row - TAPS + lax.broadcasted_iota(jnp.int32, (ROWS, 2 * TAPS), 1)).astype(F32)
    return (position >= starts).astype(F32)


def conv_block(matrix, window):
    group = lax.broadcasted_iota(jnp.int32, window.shape, 1) // GROUP
    parts = [jnp.where(group == g, window, jnp.zeros_like(window)) for g in range(LANES // GROUP)]
    return jnp.dot(matrix, jnp.concatenate(parts, axis=0), preferred_element_type=F32)


def scale_of(squares, width):
    return lax.rsqrt(jnp.sum(squares, axis=1, keepdims=True) * (1.0 / width) + 1e-06)


def device(place, row):
    return {"ctx": place, "dp": row}


def place_of(z, half, x, core):
    return ((z * 2 + half) * 4 + x) * 2 + core


def kernel(
    depth,
    chunks,
    lengths_ref,
    q_ref,
    k_ref,
    v_ref,
    gain_ref,
    filters_ref,
    bypass_ref,
    o_ref,
    att_ref,
    past_k,
    past_v,
    side_k,
    side_v,
    far_q,
    halo,
    sent_v,
    bias_ref,
    keep_ref,
    square_ref,
    base_ref,
    matrix_ref,
    r_past_k,
    r_past_v,
    r_side_k,
    r_side_v,
    r_far_q,
    r_halo,
    s_first,
    s_second,
    s_third,
    s_past_k,
    s_past_v,
    s_relay_k,
    s_relay_v,
    s_relay_h,
    s_relay_q,
):
    me, row = lax.axis_index("ctx"), lax.axis_index("dp")
    core, x, half, z = me % 2, (me // 2) % 4, (me // 8) % 2, me // 16
    other_row = (row + 2) % 4
    last, first = (x + 1) // 4, (3 - x) // 3
    mate = me + 1 - 2 * core
    left, right = core == 0, core == 1
    width = q_ref.shape[1]
    blocks = width // LANES
    per_chunk = WIDTH // LANES

    def columns(i):
        return pl.ds(pl.multiple_of(i * WIDTH, WIDTH), WIDTH)

    def onward(i, to_core):
        near = place_of(z, half, x + 1, to_core)
        relay = place_of(z, i % 2, 0, half)
        return device(near * (1 - last) + relay * last, row + last * (other_row - row)), i + last * (chunks + i // 2 - i)

    def backward(i):
        near = place_of(z, half, x - 1, 1)
        relay = place_of((z + depth - 1 + half) % depth, i % 2, 3, half)
        return device(near * (1 - first) + relay * first, row + first * (other_row - row)), i + first * (chunks + i // 2 - i)

    relay_right = device(place_of((z + core) % depth, 1 - core, 0, 1), other_row)
    relay_left = device(place_of((z + core) % depth, 1 - core, 0, 0), other_row)
    relay_back = device(place_of(z, 1 - core, 3, 1), other_row)

    def copy(source, target, send, receive, to):
        return pltpu.make_async_remote_copy(
            src_ref=source, dst_ref=target, send_sem=send, recv_sem=receive, device_id=to, device_id_type=MESH
        )

    mate_id = device(mate, row)

    def send_q(i):
        to, slot = backward(i)
        return copy(q_ref.at[:, columns(i)], far_q.at[slot], s_first.at[i], r_far_q.at[slot], to)

    def send_side_k(i):
        return copy(k_ref.at[:, columns(i)], side_k.at[i], s_second.at[i], r_side_k.at[i], mate_id)

    def send_side_v(i):
        return copy(v_ref.at[:, columns(i)], side_v.at[i], s_third.at[i], r_side_v.at[i], mate_id)

    def send_side_halo(i):
        return copy(att_ref.at[:, columns(i)], halo.at[i], s_past_k.at[i], r_halo.at[i], mate_id)

    def send_k(i):
        to, slot = onward(i, 1)
        return copy(k_ref.at[:, columns(i)], past_k.at[slot], s_first.at[i], r_past_k.at[slot], to)

    def send_v(i):
        to, slot = onward(i, 1)
        return copy(sent_v.at[i], past_v.at[slot], s_second.at[i], r_past_v.at[slot], to)

    def send_halo(i):
        to, slot = onward(i, 0)
        return copy(att_ref.at[:, columns(i)], halo.at[slot], s_third.at[i], r_halo.at[slot], to)

    def share_k(i):
        return copy(past_k.at[i], past_k.at[i], s_past_k.at[i], r_past_k.at[i], mate_id)

    def share_v(i):
        return copy(past_v.at[i], past_v.at[i], s_past_v.at[i], r_past_v.at[i], mate_id)

    def pass_k(i):
        return copy(past_k.at[chunks + i // 2], past_k.at[i], s_relay_k.at[i // 2], r_past_k.at[i], relay_right)

    def pass_v(i):
        return copy(past_v.at[chunks + i // 2], past_v.at[i], s_relay_v.at[i // 2], r_past_v.at[i], relay_right)

    def pass_halo(i):
        return copy(halo.at[chunks + i // 2], halo.at[i], s_relay_h.at[i // 2], r_halo.at[i], relay_left)

    def pass_q(i):
        return copy(far_q.at[chunks + i // 2], far_q.at[i], s_relay_q.at[i // 2], r_far_q.at[i], relay_back)

    def await_slot(buffer, receive, slot):
        copy(buffer.at[slot], buffer.at[slot], receive.at[slot], receive.at[slot], mate_id).wait_recv()

    barrier = pltpu.get_barrier_semaphore()

    def greet(place, at_row):
        pl.semaphore_signal(barrier, inc=1, device_id=device(place, at_row), device_id_type=MESH)

    greet(mate, row)
    sender = place_of((z + depth - 1 + half) % depth, 0, 0, 1 - half)

    @pl.when(x > 0)
    def _():
        greet(place_of(z, half, x - 1, 1), row)

    @pl.when(x == 0)
    def _():
        for part in range(2):
            greet(sender + 8 * part, other_row)
        greet(place_of(z, core, 3, 1), other_row)

    @pl.when(right & (x < 3))
    def _():
        greet(place_of(z, half, x + 1, 0), row)

    @pl.when(right & (x == 3))
    def _():
        for part in range(2):
            greet(place_of(z, part, 3, 1 - half), other_row)

    @pl.when(x == 3)
    def _():
        greet(place_of((z + 1 - core) % depth, core, 0, 0), other_row)

    pl.semaphore_wait(barrier, 1 + core * 2 + (1 - core) * (1 + first) + 2 * first + last)

    @pl.when(left)
    def _():
        def start(i, carry):
            send_q(i).start()
            send_side_k(i).start()
            send_side_v(i).start()
            return carry

        lax.fori_loop(0, chunks, start, 0)

    @pl.when(right)
    def _():
        def start(i, carry):
            send_k(i).start()
            return carry

        lax.fori_loop(0, chunks, start, 0)

    first_row = me * ROWS
    starts = row_starts(lengths_ref[...], first_row)
    next_first = (me + 1) * ROWS
    next_starts = row_starts(lengths_ref[...], next_first)
    keep_ref[...] = window_keeper(starts, first_row)
    base_ref[...] = filter_rows(filters_ref[...])
    square_ref[...] = jnp.zeros_like(square_ref)

    @pl.when(right)
    def _():
        bias_ref[:, : 3 * ROWS] = key_bias(starts, first_row, first_row - 2 * ROWS, 3 * ROWS)
        bias_ref[:, 3 * ROWS :] = key_bias(next_starts, next_first, next_first - 2 * ROWS, 2 * ROWS)

    short_before = (starts[0:1] >= (first_row - ROWS).astype(F32)).astype(F32)

    @pl.when(left)
    def _():
        bias_ref[:, :ROWS] = jnp.where(
            jnp.broadcast_to(short_before, (ROWS, ROWS)) > 0.5,
            key_bias(starts, first_row, first_row - ROWS, ROWS),
            MASKED,
        )
        bias_ref[:, ROWS : 2 * ROWS] = key_bias(starts, first_row, first_row, ROWS)

    next_short = (next_starts[0:1] >= (next_first - ROWS).astype(F32)).astype(F32)

    def keep_result(i, h, result):
        rounded = result.astype(BF16)
        wide = rounded.astype(F32)
        square_ref[...] += wide * wide
        att_ref[:, pl.ds(pl.multiple_of(i * WIDTH + h * HEAD_DIM, HEAD_DIM), HEAD_DIM)] = rounded

    def own_right(i):
        for h in range(CHUNK_HEADS):
            at = pl.ds(pl.multiple_of(i * WIDTH + h * HEAD_DIM, HEAD_DIM), HEAD_DIM)
            inner = slice(h * HEAD_DIM, (h + 1) * HEAD_DIM)
            keys = jnp.concatenate([past_k[i, :, inner], side_k[i, :, inner], k_ref[:, at]], axis=0)
            values = jnp.concatenate([past_v[i, :ROWS, inner], side_v[i, :, inner], v_ref[:, at]], axis=0)
            mixed, total, _ = attend(q_ref[:, at], keys, values, bias_ref[:, : 3 * ROWS])
            keep_result(i, h, mixed / total)

    def far_right(i):
        for h in range(CHUNK_HEADS):
            at = pl.ds(pl.multiple_of(i * WIDTH + h * HEAD_DIM, HEAD_DIM), HEAD_DIM)
            inner = slice(h * HEAD_DIM, (h + 1) * HEAD_DIM)
            keys = jnp.concatenate([side_k[i, :, inner], k_ref[:, at]], axis=0)
            values = jnp.concatenate([side_v[i, :, inner], v_ref[:, at]], axis=0)
            mixed, total, top = attend(far_q[i, :, inner], keys, values, bias_ref[:, 3 * ROWS :])
            level = top * EXPONENT + jnp.log2(total)
            level = jnp.where(jnp.broadcast_to(next_short, level.shape) > 0.5, MASKED, level)
            sent_v[i, :ROWS, inner] = jnp.where(
                jnp.broadcast_to(next_short, mixed.shape) > 0.5, v_ref[:, at].astype(F32), mixed / total
            ).astype(BF16)
            sent_v[i, ROWS:, inner] = pieces_of(level)

    def own_left(i):
        for h in range(CHUNK_HEADS):
            at = pl.ds(pl.multiple_of(i * WIDTH + h * HEAD_DIM, HEAD_DIM), HEAD_DIM)
            inner = slice(h * HEAD_DIM, (h + 1) * HEAD_DIM)
            keys = jnp.concatenate([past_k[i, :, inner], k_ref[:, at]], axis=0)
            values = jnp.concatenate([past_v[i, :ROWS, inner], v_ref[:, at]], axis=0)
            mixed, total, top = attend(q_ref[:, at], keys, values, bias_ref[:, : 2 * ROWS])
            far_level = column_of(past_v[i, ROWS:, inner])
            near_level = top * EXPONENT
            level = jnp.maximum(near_level, far_level)
            near_share, far_share = jnp.exp2(near_level - level), jnp.exp2(far_level - level)
            far_mixed = past_v[i, :ROWS, inner].astype(F32)
            keep_result(i, h, (near_share * mixed + far_share * far_mixed) / (near_share * total + far_share))

    def relays_q(i):
        return (x == 3) & (i < chunks) & (i % 2 == half)

    def relays_on(i):
        return (x == 0) & (i >= 0) & (i < chunks) & (i % 2 == half)

    def relay_q(i):
        @pl.when(relays_q(i))
        def _():
            await_slot(far_q, r_far_q, chunks + i // 2)
            pass_q(i).start()

    def relay_halo(i):
        @pl.when(relays_on(i))
        def _():
            await_slot(halo, r_halo, chunks + i // 2)
            pass_halo(i).start()

    relay_q(0)

    def step(i, carry):
        now = i - AHEAD
        relay_q(i + 1)

        @pl.when(relays_on(i - 1))
        def _():
            await_slot(past_k, r_past_k, chunks + (i - 1) // 2)
            pass_k(i - 1).start()

        @pl.when(relays_on(i - 2))
        def _():
            await_slot(past_v, r_past_v, chunks + (i - 2) // 2)
            pass_v(i - 2).start()

        relay_halo(now - 2)

        @pl.when(now >= 0)
        def _():
            await_slot(past_k, r_past_k, now)
            await_slot(past_v, r_past_v, now)

            @pl.when(right)
            def _():
                share_k(now).start()
                share_v(now).start()
                own_right(now)

            @pl.when(left)
            def _():
                own_left(now)

        @pl.when((i < chunks) & right)
        def _():
            await_slot(far_q, r_far_q, i)
            await_slot(side_k, r_side_k, i)
            await_slot(side_v, r_side_v, i)
            far_right(i)

        @pl.when(i < chunks)
        def _():
            for part in range(per_chunk):
                index = i * per_chunk + part
                build_block(base_ref[pl.ds(pl.multiple_of(index * 8, 8), 8), :], keep_ref[...], index, matrix_ref)

        @pl.when((i < chunks) & right)
        def _():
            send_v(i).start()

        @pl.when((now >= 0) & right)
        def _():
            send_halo(now).start()

        @pl.when((now >= 0) & left)
        def _():
            send_side_halo(now).start()

        return carry

    lax.fori_loop(0, chunks + AHEAD, step, 0)
    relay_halo(chunks - 2)
    relay_halo(chunks - 1)
    near_scale = scale_of(square_ref[...], width)

    def gather(i, total):
        await_slot(halo, r_halo, i)
        for part in range(per_chunk):
            piece = halo[i, :, part * LANES : (part + 1) * LANES].astype(F32)
            total = total + piece * piece
        return total

    far_scale = scale_of(lax.fori_loop(0, chunks, gather, jnp.zeros((ROWS, LANES), F32)), width)

    def mix(i, carry):
        for part in range(per_chunk):
            at = pl.ds(pl.multiple_of(i * WIDTH + part * LANES, LANES), LANES)
            gain = gain_ref[:, at]
            near = (att_ref[:, at].astype(F32) * near_scale * gain).astype(BF16)
            far = (halo[i, :, part * LANES : (part + 1) * LANES].astype(F32) * far_scale * gain).astype(BF16)
            summed = conv_block(matrix_ref[i * per_chunk + part], jnp.concatenate([far, near], axis=0))
            o_ref[:, at] = (summed + bypass_ref[:, at] * near.astype(F32)).astype(BF16)
        return carry

    lax.fori_loop(0, chunks, mix, 0)

    def finish(i, carry):
        @pl.when(left)
        def _():
            for sent in (send_q, send_side_k, send_side_v, send_side_halo):
                sent(i).wait_send()

        @pl.when(right)
        def _():
            for sent in (send_k, send_v, send_halo, share_k, share_v):
                sent(i).wait_send()

        @pl.when(relays_q(i))
        def _():
            pass_q(i).wait_send()

        @pl.when(relays_on(i))
        def _():
            for sent in (pass_k, pass_v, pass_halo):
                sent(i).wait_send()

        return carry

    lax.fori_loop(0, chunks, finish, 0)


def shards(mesh, queries, key_rows, value_rows, lengths, norm_gain, filters, bypass):
    width = queries.shape[1]
    chunks = width // WIDTH
    slots = chunks + chunks // 2
    vmem = pl.BlockSpec(memory_space=pltpu.VMEM)
    many = pltpu.SemaphoreType.DMA((slots,))
    some = pltpu.SemaphoreType.DMA((chunks,))
    few = pltpu.SemaphoreType.DMA((chunks // 2,))
    return pl.pallas_call(
        functools.partial(kernel, mesh.shape["ctx"] // 16, chunks),
        out_shape=jax.ShapeDtypeStruct((ROWS, width), BF16),
        in_specs=[vmem] * 7,
        out_specs=vmem,
        scratch_shapes=[
            pltpu.VMEM((ROWS, width), BF16),
            pltpu.VMEM((slots, ROWS, WIDTH), BF16),
            pltpu.VMEM((slots, ROWS + STATS, WIDTH), BF16),
            pltpu.VMEM((chunks, ROWS, WIDTH), BF16),
            pltpu.VMEM((chunks, ROWS, WIDTH), BF16),
            pltpu.VMEM((slots, ROWS, WIDTH), BF16),
            pltpu.VMEM((slots, ROWS, WIDTH), BF16),
            pltpu.VMEM((chunks, ROWS + STATS, WIDTH), BF16),
            pltpu.VMEM((ROWS, 5 * ROWS), F32),
            pltpu.VMEM((ROWS, 2 * TAPS), F32),
            pltpu.VMEM((ROWS, LANES), F32),
            pltpu.VMEM((filters.shape[0], 2 * TAPS), F32),
            pltpu.VMEM((width // LANES, ROWS, LANES // GROUP * 2 * TAPS), BF16),
            many,
            many,
            some,
            some,
            many,
            many,
            some,
            some,
            some,
            some,
            some,
            few,
            few,
            few,
            few,
        ],
        compiler_params=pltpu.CompilerParams(
            collective_id=0, has_side_effects=True, vmem_limit_bytes=56 * 2**20
        ),
        name="layer",
    )(
        lengths.reshape(1, -1),
        queries,
        key_rows,
        value_rows,
        norm_gain.reshape(1, -1),
        filters,
        bypass.reshape(1, -1),
    )


def solution(mesh):
    rows = P(("dp", "ctx"), None)
    return jax.shard_map(
        functools.partial(shards, mesh),
        mesh=mesh,
        in_specs=(rows, rows, rows, P("dp"), P(), P(), P()),
        out_specs=rows,
        check_vma=False,
    )
```

time: 217 us -> 110 us (0.51)
  the two profiles are of different devices: /device:TPU:552 before, /device:TPU:24 now
where the time goes in v2:
time: 110 us
  Pallas kernels  108 us (98%)
  local copies, waits for them, and re-layouts  2.29 us (2%)
    pallas_call x1, Pallas kernels, shards(): pl.pallas_call(functools.partial(kernel, mesh.shape['ctx'] // 16, chunks)...  108 us
    unnamed x1, local copies, waits for them, and re-layouts  2.29 us

profile of v2, /device:TPU:24, one launch (start us, length us, event | category | flops | bytes accessed | tf_op | source)
XLA Modules:
  0.0 110.2 jit_solution(1442821080407488418)
XLA Ops:
  0.0 107.9 %layer.1 = bf16[128,4096]{1,0:T(8,128)(2,1)} custom-call(s32[1,128]{1,0:T(1,128)} %bitcast.5, bf16[128,4096]{1,0:T(8,128)(2,1)} %q_ref.1, bf16[128,4096]{1,0:T(8,128)(2,1)} %k_ref.1, bf16[128,4096]{1,0:T(8,128)(2,1)} %v_ref.1, f32[1,4096]{1,0:T(1,128)} %bitcast.3, bf16[256,128]{1,0:T(8,128)(2,1)} %filters_ref.1, f32[1,4096]{1,0:T(1,128)} %bitcast.4), custom_call_target="tpu_custom_call" | custom-call | tf_op jit(solution)/shard_map/layer/pallas_call | solution.py:489
  107.9 2.3 %copy.9 = bf16[128,4096]{1,0:T(8,128)(2,1)} copy(bf16[128,4096]{1,0:T(8,128)(2,1)} %layer.1) | data formatting | bytes 2097152

commit v3 on v2

--- a/solution.py
+++ b/solution.py
@@ -16,11 +16,12 @@
 STATS = 16
 CHUNK_HEADS = 2
 WIDTH = CHUNK_HEADS * HEAD_DIM
-AHEAD = 4
 F32 = jnp.float32
 BF16 = jnp.bfloat16
 EXPONENT = math.log2(math.e) / math.sqrt(HEAD_DIM)
 MASKED = -1e30
+OWN_LAG = 6
+HALO_LAG = 10
 MESH = pl.DeviceIdType.MESH
 
 
@@ -47,8 +48,9 @@
     scores = lax.dot_general(query, keys, (((1,), (1,)), ((), ())), preferred_element_type=F32) + bias
     top = jnp.max(scores, axis=1, keepdims=True)
     raised = jnp.exp2((scores - top) * EXPONENT)
-    total = jnp.sum(raised, axis=1, keepdims=True)
-    return jnp.dot(raised.astype(BF16), values, preferred_element_type=F32), total, top
+    rounded = raised.astype(BF16)
+    summed = jnp.dot(rounded, jnp.concatenate([values, jnp.ones_like(values)], axis=1), preferred_element_type=F32)
+    return summed[:, :HEAD_DIM], summed[:, HEAD_DIM:], top
 
 
 def diagonal():
@@ -103,10 +105,6 @@
 
 def device(place, row):
     return {"ctx": place, "dp": row}
-
-
-def place_of(z, half, x, core):
-    return ((z * 2 + half) * 4 + x) * 2 + core
 
 
 def kernel(
@@ -150,10 +148,11 @@
     s_relay_q,
 ):
     me, row = lax.axis_index("ctx"), lax.axis_index("dp")
-    core, x, half, z = me % 2, (me // 2) % 4, (me // 8) % 2, me // 16
-    other_row = (row + 2) % 4
+    core, x = me % 2, (me // 2) % 4
+    chip, chips = me // 2, depth * 8
     last, first = (x + 1) // 4, (3 - x) // 3
     mate = me + 1 - 2 * core
+    next_chip, past_chip = (chip + 1) % chips, (chip + chips - 1) % chips
     left, right = core == 0, core == 1
     width = q_ref.shape[1]
     blocks = width // LANES
@@ -162,19 +161,25 @@
     def columns(i):
         return pl.ds(pl.multiple_of(i * WIDTH, WIDTH), WIDTH)
 
+    head, tail = chip == 0, chip == chips - 1
+    turn = 1 + (2 * x) % 3
+    row_last = chip - x + 3
+
     def onward(i, to_core):
-        near = place_of(z, half, x + 1, to_core)
-        relay = place_of(z, i % 2, 0, half)
-        return device(near * (1 - last) + relay * last, row + last * (other_row - row)), i + last * (chunks + i // 2 - i)
+        relayed = last * ((i % 4 + 2) // 3)
+        place = 2 * next_chip + to_core
+        relay = 2 * (chip - 3 + (2 * (i % 4) + 1) % 3)
+        return device(place + relayed * (relay - place), row), i + relayed * (chunks + i // 4 - i)
 
     def backward(i):
-        near = place_of(z, half, x - 1, 1)
-        relay = place_of((z + depth - 1 + half) % depth, i % 2, 3, half)
-        return device(near * (1 - first) + relay * first, row + first * (other_row - row)), i + first * (chunks + i // 2 - i)
-
-    relay_right = device(place_of((z + core) % depth, 1 - core, 0, 1), other_row)
-    relay_left = device(place_of((z + core) % depth, 1 - core, 0, 0), other_row)
-    relay_back = device(place_of(z, 1 - core, 3, 1), other_row)
+        relayed = first * (i % 2)
+        place = 2 * past_chip + 1
+        return device(place + relayed * (2 * (chip + 3) - place), row), i + relayed * (chunks + i // 2 - i)
+
+    def relay_target(to_core):
+        return device(2 * ((row_last + 1) % chips) + to_core, row)
+
+    relay_back = device(2 * ((chip + chips - 4) % chips) + 1, row)
 
     def copy(source, target, send, receive, to):
         return pltpu.make_async_remote_copy(
@@ -214,71 +219,93 @@
     def share_v(i):
         return copy(past_v.at[i], past_v.at[i], s_past_v.at[i], r_past_v.at[i], mate_id)
 
+    def pass_on(buffer, send, receive, i, to, share=4):
+        return copy(buffer.at[chunks + i // share], buffer.at[i], send.at[i // share], receive.at[i], to)
+
     def pass_k(i):
-        return copy(past_k.at[chunks + i // 2], past_k.at[i], s_relay_k.at[i // 2], r_past_k.at[i], relay_right)
+        return pass_on(past_k, s_relay_k, r_past_k, i, relay_target(1))
 
     def pass_v(i):
-        return copy(past_v.at[chunks + i // 2], past_v.at[i], s_relay_v.at[i // 2], r_past_v.at[i], relay_right)
+        return pass_on(past_v, s_relay_v, r_past_v, i, relay_target(1))
 
     def pass_halo(i):
-        return copy(halo.at[chunks + i // 2], halo.at[i], s_relay_h.at[i // 2], r_halo.at[i], relay_left)
+        return pass_on(halo, s_relay_h, r_halo, i, relay_target(0))
 
     def pass_q(i):
-        return copy(far_q.at[chunks + i // 2], far_q.at[i], s_relay_q.at[i // 2], r_far_q.at[i], relay_back)
+        return pass_on(far_q, s_relay_q, r_far_q, i, relay_back, 2)
 
     def await_slot(buffer, receive, slot):
         copy(buffer.at[slot], buffer.at[slot], receive.at[slot], receive.at[slot], mate_id).wait_recv()
 
     barrier = pltpu.get_barrier_semaphore()
 
-    def greet(place, at_row):
-        pl.semaphore_signal(barrier, inc=1, device_id=device(place, at_row), device_id_type=MESH)
-
-    greet(mate, row)
-    sender = place_of((z + depth - 1 + half) % depth, 0, 0, 1 - half)
-
-    @pl.when(x > 0)
-    def _():
-        greet(place_of(z, half, x - 1, 1), row)
+    def greet(place):
+        pl.semaphore_signal(barrier, inc=1, device_id=device(place, row), device_id_type=MESH)
+
+    greet(mate)
+    greet(2 * past_chip + 1)
 
     @pl.when(x == 0)
     def _():
-        for part in range(2):
-            greet(sender + 8 * part, other_row)
-        greet(place_of(z, core, 3, 1), other_row)
-
-    @pl.when(right & (x < 3))
-    def _():
-        greet(place_of(z, half, x + 1, 0), row)
+        for part in range(3):
+            greet(2 * ((chip + chips - 4 + part) % chips))
+
+    @pl.when(right)
+    def _():
+        greet(2 * next_chip)
 
     @pl.when(right & (x == 3))
     def _():
-        for part in range(2):
-            greet(place_of(z, part, 3, 1 - half), other_row)
-
-    @pl.when(x == 3)
-    def _():
-        greet(place_of((z + 1 - core) % depth, core, 0, 0), other_row)
-
-    pl.semaphore_wait(barrier, 1 + core * 2 + (1 - core) * (1 + first) + 2 * first + last)
+        greet(2 * ((chip + 4) % chips))
+
+    @pl.when(left & (x < 3))
+    def _():
+        greet(2 * row_last + 1)
+
+    @pl.when(left & (x == 3))
+    def _():
+        greet(2 * (chip - 3))
+
+    pl.semaphore_wait(barrier, core * (3 + 3 * last) + (1 - core) * (4 + first - last))
 
     @pl.when(left)
     def _():
         def start(i, carry):
-            send_q(i).start()
+            @pl.when(chip > 0)
+            def _():
+                send_q(i).start()
+
             send_side_k(i).start()
             send_side_v(i).start()
             return carry
 
         lax.fori_loop(0, chunks, start, 0)
 
-    @pl.when(right)
+    @pl.when(right & (chip < chips - 1))
     def _():
         def start(i, carry):
             send_k(i).start()
             return carry
 
         lax.fori_loop(0, chunks, start, 0)
+
+    @pl.when(right & head)
+    def _():
+        def clear(i, carry):
+            past_k[i] = jnp.zeros(past_k.shape[1:], BF16)
+            past_v[i, :ROWS] = jnp.zeros((ROWS, WIDTH), BF16)
+            past_v[i, ROWS:] = jnp.full((STATS, WIDTH), MASKED, BF16)
+            return carry
+
+        lax.fori_loop(0, chunks, clear, 0)
+
+    @pl.when(left & head)
+    def _():
+        def clear(i, carry):
+            halo[i] = jnp.zeros(halo.shape[1:], BF16)
+            return carry
+
+        lax.fori_loop(0, chunks, clear, 0)
 
     first_row = me * ROWS
     starts = row_starts(lengths_ref[...], first_row)
@@ -350,90 +377,114 @@
             keep_result(i, h, (near_share * mixed + far_share * far_mixed) / (near_share * total + far_share))
 
     def relays_q(i):
-        return (x == 3) & (i < chunks) & (i % 2 == half)
+        return left & (x == 3) & (chip > 3) & (i % 2 == 1)
 
     def relays_on(i):
-        return (x == 0) & (i >= 0) & (i < chunks) & (i % 2 == half)
-
-    def relay_q(i):
-        @pl.when(relays_q(i))
-        def _():
-            await_slot(far_q, r_far_q, chunks + i // 2)
-            pass_q(i).start()
-
-    def relay_halo(i):
-        @pl.when(relays_on(i))
-        def _():
-            await_slot(halo, r_halo, chunks + i // 2)
-            pass_halo(i).start()
-
-    relay_q(0)
-
-    def step(i, carry):
-        now = i - AHEAD
-        relay_q(i + 1)
-
-        @pl.when(relays_on(i - 1))
-        def _():
-            await_slot(past_k, r_past_k, chunks + (i - 1) // 2)
-            pass_k(i - 1).start()
-
-        @pl.when(relays_on(i - 2))
-        def _():
-            await_slot(past_v, r_past_v, chunks + (i - 2) // 2)
-            pass_v(i - 2).start()
-
-        relay_halo(now - 2)
-
-        @pl.when(now >= 0)
-        def _():
-            await_slot(past_k, r_past_k, now)
-            await_slot(past_v, r_past_v, now)
-
-            @pl.when(right)
-            def _():
-                share_k(now).start()
-                share_v(now).start()
-                own_right(now)
-
-            @pl.when(left)
-            def _():
+        return left & (x < 3) & (row_last < chips - 1) & (i % 4 == turn)
+
+    def build(i):
+        for part in range(per_chunk):
+            index = i * per_chunk + part
+            build_block(base_ref[pl.ds(pl.multiple_of(index * 8, 8), 8), :], keep_ref[...], index, matrix_ref)
+
+    @pl.when(right)
+    def _():
+        @pl.when(chip < chips - 1)
+        def _():
+            def early(i, carry):
+                await_slot(far_q, r_far_q, i)
+                await_slot(side_k, r_side_k, i)
+                await_slot(side_v, r_side_v, i)
+                far_right(i)
+                send_v(i).start()
+                return carry
+
+            lax.fori_loop(0, chunks, early, 0)
+
+        @pl.when(tail)
+        def _():
+            def early(i, carry):
+                await_slot(side_k, r_side_k, i)
+                await_slot(side_v, r_side_v, i)
+                return carry
+
+            lax.fori_loop(0, chunks, early, 0)
+
+        def late(i, carry):
+            @pl.when(chip > 0)
+            def _():
+                await_slot(past_k, r_past_k, i)
+                await_slot(past_v, r_past_v, i)
+
+            share_k(i).start()
+            share_v(i).start()
+            own_right(i)
+
+            @pl.when(chip < chips - 1)
+            def _():
+                send_halo(i).start()
+
+            return carry
+
+        lax.fori_loop(0, chunks, late, 0)
+
+        def rest(i, carry):
+            build(i)
+            return carry
+
+        lax.fori_loop(0, chunks, rest, 0)
+
+    @pl.when(left)
+    def _():
+        def early(i, carry):
+            @pl.when(relays_q(i))
+            def _():
+                await_slot(far_q, r_far_q, chunks + i // 2)
+                pass_q(i).start()
+
+            @pl.when(relays_on(i))
+            def _():
+                await_slot(past_k, r_past_k, chunks + i // 4)
+                pass_k(i).start()
+
+            build(i)
+            return carry
+
+        lax.fori_loop(0, chunks, early, 0)
+
+        def late(step, carry):
+            @pl.when((step < chunks) & relays_on(step))
+            def _():
+                await_slot(past_v, r_past_v, chunks + step // 4)
+                pass_v(step).start()
+
+            now = step - OWN_LAG
+
+            @pl.when((now >= 0) & (now < chunks))
+            def _():
+                await_slot(past_k, r_past_k, now)
+                await_slot(past_v, r_past_v, now)
                 own_left(now)
-
-        @pl.when((i < chunks) & right)
-        def _():
-            await_slot(far_q, r_far_q, i)
-            await_slot(side_k, r_side_k, i)
-            await_slot(side_v, r_side_v, i)
-            far_right(i)
-
-        @pl.when(i < chunks)
-        def _():
-            for part in range(per_chunk):
-                index = i * per_chunk + part
-                build_block(base_ref[pl.ds(pl.multiple_of(index * 8, 8), 8), :], keep_ref[...], index, matrix_ref)
-
-        @pl.when((i < chunks) & right)
-        def _():
-            send_v(i).start()
-
-        @pl.when((now >= 0) & right)
-        def _():
-            send_halo(now).start()
-
-        @pl.when((now >= 0) & left)
-        def _():
-            send_side_halo(now).start()
-
-        return carry
-
-    lax.fori_loop(0, chunks + AHEAD, step, 0)
-    relay_halo(chunks - 2)
-    relay_halo(chunks - 1)
+                send_side_halo(now).start()
+
+            past = step - HALO_LAG
+
+            @pl.when((past >= 0) & relays_on(past))
+            def _():
+                await_slot(halo, r_halo, chunks + past // 4)
+                pass_halo(past).start()
+
+            return carry
+
+        lax.fori_loop(0, chunks + HALO_LAG, late, 0)
+
     near_scale = scale_of(square_ref[...], width)
 
     def gather(i, total):
-        await_slot(halo, r_halo, i)
+        @pl.when(right | (chip > 0))
+        def _():
+            await_slot(halo, r_halo, i)
+
         for part in range(per_chunk):
             piece = halo[i, :, part * LANES : (part + 1) * LANES].astype(F32)
             total = total + piece * piece
@@ -456,12 +507,21 @@
     def finish(i, carry):
         @pl.when(left)
         def _():
-            for sent in (send_q, send_side_k, send_side_v, send_side_halo):
+            for sent in (send_side_k, send_side_v, send_side_halo):
                 sent(i).wait_send()
 
+        @pl.when(left & (chip > 0))
+        def _():
+            send_q(i).wait_send()
+
         @pl.when(right)
         def _():
-            for sent in (send_k, send_v, send_halo, share_k, share_v):
+            for sent in (share_k, share_v):
+                sent(i).wait_send()
+
+        @pl.when(right & (chip < chips - 1))
+        def _():
+            for sent in (send_k, send_v, send_halo):
                 sent(i).wait_send()
 
         @pl.when(relays_q(i))

time: 110 us -> 80.8 us (0.73)
  the two profiles are of different devices: /device:TPU:24 before, /device:TPU:41 now
where the time goes in v3:
time: 80.8 us; the launch traced here: 80.7 us
  Pallas kernels  78.4 us (97%)
  local copies, waits for them, and re-layouts  2.29 us (3%)
    pallas_call x1, Pallas kernels, shards(): pl.pallas_call(functools.partial(kernel, mesh.shape['ctx'] // 16, chunks)...  78.4 us
    unnamed x1, local copies, waits for them, and re-layouts  2.29 us

profile of v3, /device:TPU:41, one launch (start us, length us, event | category | flops | bytes accessed | tf_op | source)
XLA Modules:
  0.0 80.7 jit_solution(3118275098996230825)
XLA Ops:
  0.0 78.4 %layer.1 = bf16[128,4096]{1,0:T(8,128)(2,1)} custom-call(s32[1,128]{1,0:T(1,128)} %bitcast.5, bf16[128,4096]{1,0:T(8,128)(2,1)} %q_ref.1, bf16[128,4096]{1,0:T(8,128)(2,1)} %k_ref.1, bf16[128,4096]{1,0:T(8,128)(2,1)} %v_ref.1, f32[1,4096]{1,0:T(1,128)} %bitcast.3, bf16[256,128]{1,0:T(8,128)(2,1)} %filters_ref.1, f32[1,4096]{1,0:T(1,128)} %bitcast.4), custom_call_target="tpu_custom_call" | custom-call | tf_op jit(solution)/shard_map/layer/pallas_call | solution.py:549
  78.4 2.3 %copy.9 = bf16[128,4096]{1,0:T(8,128)(2,1)} copy(bf16[128,4096]{1,0:T(8,128)(2,1)} %layer.1) | data formatting | bytes 2097152

commit v4 on v3

--- a/solution.py
+++ b/solution.py
@@ -172,14 +172,15 @@
         return device(place + relayed * (relay - place), row), i + relayed * (chunks + i // 4 - i)
 
     def backward(i):
-        relayed = first * (i % 2)
+        relayed = first * ((i % 4 + 2) // 3)
         place = 2 * past_chip + 1
-        return device(place + relayed * (2 * (chip + 3) - place), row), i + relayed * (chunks + i // 2 - i)
+        relay = 2 * (chip + 1 + (2 * (i % 4)) % 3)
+        return device(place + relayed * (relay - place), row), i + relayed * (chunks + i // 4 - i)
 
     def relay_target(to_core):
         return device(2 * ((row_last + 1) % chips) + to_core, row)
 
-    relay_back = device(2 * ((chip + chips - 4) % chips) + 1, row)
+    relay_back = device(2 * ((chip - x + chips - 1) % chips) + 1, row)
 
     def copy(source, target, send, receive, to):
         return pltpu.make_async_remote_copy(
@@ -232,7 +233,7 @@
         return pass_on(halo, s_relay_h, r_halo, i, relay_target(0))
 
     def pass_q(i):
-        return pass_on(far_q, s_relay_q, r_far_q, i, relay_back, 2)
+        return pass_on(far_q, s_relay_q, r_far_q, i, relay_back)
 
     def await_slot(buffer, receive, slot):
         copy(buffer.at[slot], buffer.at[slot], receive.at[slot], receive.at[slot], mate_id).wait_recv()
@@ -256,17 +257,18 @@
 
     @pl.when(right & (x == 3))
     def _():
-        greet(2 * ((chip + 4) % chips))
+        for part in range(3):
+            greet(2 * ((chip + 2 + part) % chips))
 
     @pl.when(left & (x < 3))
     def _():
         greet(2 * row_last + 1)
 
-    @pl.when(left & (x == 3))
-    def _():
-        greet(2 * (chip - 3))
-
-    pl.semaphore_wait(barrier, core * (3 + 3 * last) + (1 - core) * (4 + first - last))
+    @pl.when(left & (x > 0))
+    def _():
+        greet(2 * (chip - x))
+
+    pl.semaphore_wait(barrier, core * (3 + 3 * last) + (1 - core) * (5 + 2 * first - 2 * last))
 
     @pl.when(left)
     def _():
@@ -377,7 +379,7 @@
             keep_result(i, h, (near_share * mixed + far_share * far_mixed) / (near_share * total + far_share))
 
     def relays_q(i):
-        return left & (x == 3) & (chip > 3) & (i % 2 == 1)
+        return left & (x > 0) & (chip > x) & (i % 4 == 4 - x)
 
     def relays_on(i):
         return left & (x < 3) & (row_last < chips - 1) & (i % 4 == turn)
@@ -439,7 +441,7 @@
         def early(i, carry):
             @pl.when(relays_q(i))
             def _():
-                await_slot(far_q, r_far_q, chunks + i // 2)
+                await_slot(far_q, r_far_q, chunks + i // 4)
                 pass_q(i).start()
 
             @pl.when(relays_on(i))

time: 80.8 us -> 80.9 us (level)
  no operation moved by 1% of the time
where the time goes in v4:
time: 80.9 us; the launch traced here: 80.7 us
  Pallas kernels  78.4 us (97%)
  local copies, waits for them, and re-layouts  2.29 us (3%)
    pallas_call x1, Pallas kernels, shards(): pl.pallas_call(functools.partial(kernel, mesh.shape['ctx'] // 16, chunks)...  78.4 us
    unnamed x1, local copies, waits for them, and re-layouts  2.29 us

profile of v4, /device:TPU:41, one launch (start us, length us, event | category | flops | bytes accessed | tf_op | source)
XLA Modules:
  0.0 80.7 jit_solution(4253488428776768508)
XLA Ops:
  0.0 78.4 %layer.1 = bf16[128,4096]{1,0:T(8,128)(2,1)} custom-call(s32[1,128]{1,0:T(1,128)} %bitcast.5, bf16[128,4096]{1,0:T(8,128)(2,1)} %q_ref.1, bf16[128,4096]{1,0:T(8,128)(2,1)} %k_ref.1, bf16[128,4096]{1,0:T(8,128)(2,1)} %v_ref.1, f32[1,4096]{1,0:T(1,128)} %bitcast.3, bf16[256,128]{1,0:T(8,128)(2,1)} %filters_ref.1, f32[1,4096]{1,0:T(1,128)} %bitcast.4), custom_call_target="tpu_custom_call" | custom-call | tf_op jit(solution)/shard_map/layer/pallas_call | solution.py:551
  78.4 2.3 %copy.9 = bf16[128,4096]{1,0:T(8,128)(2,1)} copy(bf16[128,4096]{1,0:T(8,128)(2,1)} %layer.1) | data formatting | bytes 2097152
